TPU v7x, 32 devices: a whole 2x2x4 slice. The times are simulated.
32 devices in a mesh: row: 4 (over y, core), col: 8 (over z, x).
Axes of the slice: x: 2, y: 2, z: 4, core: 2. Of those that a mesh axis runs over, the one named last changes fastest.
Arguments:
- left: bfloat16 [128, 8192], P('col', 'row'), may hold values from -6 to 6
- right: bfloat16 [128, 8192], P('row', 'col'), may hold values from -6 to 6
- proj: bfloat16 [1024, 128], replicated, may hold values from -2 to 2
- bias: float32 [128], replicated, may hold values from -1 to 1
- pair_grad: bfloat16 [256, 256, 128], P('row', 'col'), may hold values from -0.1875 to 0.1875
Outputs:
- pair_out: bfloat16 [256, 256, 128], P('row', 'col')
- left_grad: float32 [128, 8192], P('col', 'row')
- right_grad: float32 [128, 8192], P('row', 'col')
- proj_grad: float32 [1024, 128], replicated
All inputs are finite; a program needn't handle non-finite values.
Results may differ from a plain program's by a relative error of at most 0.0056.
Values may be sent and summed in bfloat16 or wider, within the bound.
A program may use at most 128 MiB of HBM per device.

v0:
```python
import jax
import jax.numpy as jnp
from jax import lax
from jax.sharding import PartitionSpec as P

CH = 32
PAIR = 128
SEQS = 128
OUTER = 1024


def shards(left, right, proj, bias, pair_grad):
    left_all = lax.all_gather(left, "col", axis=0, tiled=True)
    right_all = lax.all_gather(right, "row", axis=0, tiled=True)
    seq_count = left_all.shape[0]
    rows_here = left_all.shape[1] // CH
    cols_here = right_all.shape[1] // CH
    left_cube = left_all.reshape(seq_count, rows_here, CH)
    right_cube = right_all.reshape(seq_count, cols_here, CH)
    square = (
        jnp.einsum("sic,sje->ijce", left_cube, right_cube, preferred_element_type=jnp.float32)
        / SEQS
    )
    outers = square.astype(jnp.bfloat16).reshape(rows_here * cols_here, OUTER)
    preact = jnp.dot(outers, proj, preferred_element_type=jnp.float32) + bias
    active = jnp.maximum(preact, 0.0)
    pair_out = (active * active).astype(jnp.bfloat16).reshape(rows_here, cols_here, PAIR)
    grad_pre = (
        pair_grad.reshape(rows_here * cols_here, PAIR).astype(jnp.float32) * 2.0 * active
    ).astype(jnp.bfloat16)
    weight_term = lax.dot_general(
        outers, grad_pre, (((0,), (0,)), ((), ())), preferred_element_type=jnp.float32
    )
    proj_grad = lax.psum(weight_term, ("row", "col"))
    grad_outer = jnp.dot(grad_pre, proj.T, preferred_element_type=jnp.float32).astype(jnp.bfloat16)
    grad_cube = grad_outer.reshape(rows_here, cols_here, CH, CH)
    left_whole = (
        jnp.einsum("ijce,sje->sic", grad_cube, right_cube, preferred_element_type=jnp.float32)
        / SEQS
    )
    right_whole = (
        jnp.einsum("ijce,sic->sje", grad_cube, left_cube, preferred_element_type=jnp.float32) / SEQS
    )
    left_grad = lax.psum_scatter(
        left_whole.reshape(seq_count, rows_here * CH), "col", scatter_dimension=0, tiled=True
    )
    right_grad = lax.psum_scatter(
        right_whole.reshape(seq_count, cols_here * CH), "row", scatter_dimension=0, tiled=True
    )
    return (pair_out, left_grad, right_grad, proj_grad)


def solution(mesh):
    return jax.shard_map(
        shards,
        mesh=mesh,
        in_specs=(P("col", "row"), P("row", "col"), P(), P(), P("row", "col", None)),
        out_specs=(P("row", "col", None), P("col", "row"), P("row", "col"), P()),
        check_vma=False,
    )
```

profile of v0, /device:TPU:0, one launch (start us, length us, event | category | flops | bytes accessed | tf_op | source)
XLA Modules:
  0.0 248.4 jit_solution(3948851120335303654)
XLA Ops:
  8.0 0.0 all-reduce.2.cloned.1.call-start
  8.1 33.4 %all_gather.7 = bf16[128,2048]{1,0:T(8,128)(2,1)S(1)} all-gather(bf16[16,2048]{1,0:T(8,128)(2,1)} %param.5), channel_id=1, replica_groups=mesh['row'=4,'col'=8] {'col'}, dimensions={0}, use_global_device_ids=true | all-gather | bytes 589824 | tf_op jit(solution)/shard_map/all_gather | solution.py:13
  41.4 0.3 copy.26
  41.7 6.0 %all_gather.6 = bf16[128,1024]{1,0:T(8,128)(2,1)S(1)} all-gather(bf16[32,1024]{1,0:T(8,128)(2,1)} %param.6), channel_id=1, replica_groups=mesh['row'=4,'col'=8] {'row'}, dimensions={0}, use_global_device_ids=true | all-gather | bytes 327680 | tf_op jit(solution)/shard_map/all_gather | solution.py:14
  47.7 0.2 copy.25
  47.9 5.6 %fusion = bf16[64,32,32,32]{0,3,2,1:T(8,128)(2,1)} fusion(bf16[128,32,32,1]{0,2,3,1:T(8,128)(2,1)S(1)} %bitcast.50, bf16[128,64,32]{0,2,1:T(8,128)(2,1)S(1)} %bitcast.48), kind=kOutput, calls=%fused_computation.1 | convolution fusion | flops 541065216 | bytes 4980736 | tf_op jit(solution)/shard_map/sic,sje->ijce/dot_general | solution.py:21
  53.5 24.6 %copy.28 = bf16[64,32,32,32]{3,2,1,0:T(8,128)(2,1)} copy(bf16[64,32,32,32]{0,3,2,1:T(8,128)(2,1)} %fusion) | data formatting | bytes 8388608 | tf_op jit(solution)/shard_map/convert_element_type | solution.py:24
  78.1 23.3 %reshape.36 = bf16[2048,1024]{1,0:T(8,128)(2,1)} reshape(bf16[64,32,32,32]{3,2,1,0:T(8,128)(2,1)} %copy.28) | data formatting | bytes 8388608 | tf_op jit(solution)/shard_map/reshape | solution.py:24
  101.4 0.1 convert_multiply_fusion
  101.6 4.4 %fusion.4 = (bf16[2048,128]{1,0:T(8,128)(2,1)S(1)}, bf16[2048,128]{1,0:T(8,128)(2,1)}) fusion(f32[64,32,128]{2,1,0:T(8,128)S(1)} %convert_multiply_fusion, f32[128]{0:T(128)S(1)} %copy-done.3, bf16[2048,1024]{1,0:T(8,128)(2,1)} %reshape.36, bf16[1024,128]{1,0:T(8,128)(2,1)S(1)} %copy-done), kind=kOutput, calls=%fused_computation.10 | convolution fusion | flops 538443776 | bytes 6554112 | tf_op jit(solution)/shard_map/dot_general | solution.py:25
  106.0 2.1 fusion.7
  108.1 0.0 all-reduce.2.cloned.1.call-update
  108.1 0.2 reduce-scatter.5.cloned.1.call-start
  108.3 3.2 %convolution_convert_fusion = bf16[2048,1024]{1,0:T(8,128)(2,1)} fusion(bf16[2048,128]{1,0:T(8,128)(2,1)S(1)} %get-tuple-element.4, bf16[1024,128]{1,0:T(8,128)(2,1)S(1)} %copy-done), kind=kOutput, calls=%fused_computation.2 | convolution fusion | flops 538968064 | bytes 4980736 | tf_op jit(solution)/shard_map/dot_general | solution.py:35
  111.5 20.3 %reshape.38 = bf16[64,32,32,32]{3,2,1,0:T(8,128)(2,1)} reshape(bf16[2048,1024]{1,0:T(8,128)(2,1)} %convolution_convert_fusion) | data formatting | bytes 8388608 | tf_op jit(solution)/shard_map/reshape | solution.py:36
  131.9 10.3 %fusion.3 = f32[32,32,128]{2,1,0:T(8,128)S(1)} fusion(bf16[64,32,32,32]{3,2,1,0:T(8,128)(2,1)} %reshape.38, bf16[128,64,32,1]{0,2,3,1:T(8,128)(2,1)S(1)} %bitcast.49), kind=kOutput, calls=%fused_computation.8 | convolution fusion | flops 537001984 | bytes 5242880 | tf_op jit(solution)/shard_map/ijce,sic->sje/dot_general | solution.py:42
  142.2 1.0 copy.31
  143.2 0.0 reduce-scatter.5.cloned.1.call-update
  143.2 0.0 reduce-scatter.3.cloned.1.call-start
  143.3 9.1 %fusion.2 = f32[64,32,128]{2,1,0:T(8,128)S(1)} fusion(bf16[64,32,32,32]{3,2,1,0:T(8,128)(2,1)} %reshape.38, bf16[128,32,32,1]{0,2,1,3:T(8,128)(2,1)S(1)} %bitcast.51), kind=kOutput, calls=%fused_computation.6 | convolution fusion | flops 537133056 | bytes 5505024 | tf_op jit(solution)/shard_map/ijce,sje->sic/dot_general | solution.py:38
  152.4 1.3 copy.29
  153.7 0.0 reduce-scatter.3.cloned.1.call-update
  153.8 85.4 %all-reduce.2.cloned.1.call-done = f32[1024,128]{1,0:T(8,128)} async-done(((f32[1024,128]{1,0:T(8,128)}), f32[1024,128]{1,0:T(8,128)}) %all-reduce.2.cloned.1.call-update) | async-done | bytes 524304 | tf_op jit(solution)/shard_map/psum | solution.py:34
  239.1 1.9 copy.41
  (10 shorter events, 0.0 us)
Async XLA Ops:
  8.0 93.6 %copy-start = (bf16[1024,128]{1,0:T(8,128)(2,1)S(1)}, bf16[1024,128]{1,0:T(8,128)(2,1)}, u32[]{:S(2)}) copy-start(bf16[1024,128]{1,0:T(8,128)(2,1)} %param.7) | copy-start | bytes 786436
  8.0 231.1 %all-reduce.2.cloned.1.call-start = ((), (), s32[]{:S(2)}) async-start(), calls=%async_computation.4 | async-start | bytes 1048576 | tf_op jit(solution)/shard_map/psum | solution.py:34
  78.1 23.3 %copy-start.2 = (bf16[64,32,128]{2,1,0:T(8,128)(2,1)S(1)}, bf16[64,32,128]{2,1,0:T(8,128)(2,1)}, u32[]{:S(2)}) copy-start(bf16[64,32,128]{2,1,0:T(8,128)(2,1)} %param.9) | copy-start | bytes 1572868
  78.1 23.5 %copy-start.3 = (f32[128]{0:T(128)S(1)}, f32[128]{0:T(128)}, u32[]{:S(2)}) copy-start(f32[128]{0:T(128)} %param.8) | copy-start | bytes 1540
  101.4 4.5 %copy-start.1 = (bf16[2048,1024]{1,0:T(8,128)(2,1)S(1)}, bf16[2048,1024]{1,0:T(8,128)(2,1)}, u32[]{:S(2)}) copy-start(bf16[2048,1024]{1,0:T(8,128)(2,1)} %reshape.36) | copy-start | bytes 12582916
  108.1 131.0 %reduce-scatter.5.cloned.1.call-start = ((), (), s32[]{:S(2)}) async-start(), calls=%async_computation.3 | async-start | bytes 655360 | tf_op jit(solution)/shard_map/reduce_scatter | solution.py:47
  143.2 95.9 %reduce-scatter.3.cloned.1.call-start = ((), (), s32[]{:S(2)}) async-start(), calls=%async_computation.2 | async-start | bytes 1179648 | tf_op jit(solution)/shard_map/reduce_scatter | solution.py:44
Sparse Core Ops, SparseCore 0:
  108.2 130.8 all-reduce.1
Sparse Core Ops, SparseCore 1:
  143.3 22.7 reduce-scatter.4
  169.9 64.3 reduce-scatter.2
where the time goes:
time: 250 us; the launch traced here: 248 us
  waiting for transfers between devices  85.4 us (34%)
  local copies, waits for them, and re-layouts  72.9 us (29%)
  blocking collectives  39.4 us (16%)
  matrix products  34.8 us (14%)
  between operations  15.5 us (6%)
    psum x1, waiting for transfers between devices, shards(): proj_grad = lax.psum(weight_term, ('row', 'col'))  85.4 us
    all_gather x1, blocking collectives, shards(): left_all = lax.all_gather(left, 'col', axis=0, tiled=True)  33.4 us
    convert_element_type x1, local copies, waits for them, and re-layouts, shards(): outers = square.astype(jnp.bfloat16).reshape(rows_here * cols_here, OUTER)  24.6 us
    reshape x1, local copies, waits for them, and re-layouts, shards(): outers = square.astype(jnp.bfloat16).reshape(rows_here * cols_here, OUTER)  23.3 us
    reshape x1, local copies, waits for them, and re-layouts, shards(): grad_cube = grad_outer.reshape(rows_here, cols_here, CH, CH)  20.3 us
    dot_general x1, matrix products, shards(): jnp.einsum('ijce,sic->sje', grad_cube, left_cube, preferred_element_type=...  10.3 us
    dot_general x1, matrix products, shards(): jnp.einsum('ijce,sje->sic', grad_cube, right_cube, preferred_element_type...  9.14 us
    all_gather x1, blocking collectives, shards(): right_all = lax.all_gather(right, 'row', axis=0, tiled=True)  5.99 us
  transfers between devices with their start and end apart: 3, of which 1 were waited for; matrix products, arithmetic and copies ran while one was open for 18% of the time, Pallas kernels for 0%

commit v1 on v0

--- a/solution.py
+++ b/solution.py
@@ -2,11 +2,18 @@
 import jax.numpy as jnp
 from jax import lax
 from jax.sharding import PartitionSpec as P
+from jax.lax import all_gather
 
 CH = 32
 PAIR = 128
 SEQS = 128
 OUTER = 1024
+
+
+def carry_weights(row_axis, shard_in):
+    odd = all_gather(shard_in, axis_name=row_axis)
+    y = jnp.sum(odd, axis=0)
+    return y
 
 
 def shards(left, right, proj, bias, pair_grad):
@@ -31,7 +38,7 @@
     weight_term = lax.dot_general(
         outers, grad_pre, (((0,), (0,)), ((), ())), preferred_element_type=jnp.float32
     )
-    proj_grad = lax.psum(weight_term, ("row", "col"))
+    proj_grad = carry_weights(("row", "col"), weight_term)
     grad_outer = jnp.dot(grad_pre, proj.T, preferred_element_type=jnp.float32).astype(jnp.bfloat16)
     grad_cube = grad_outer.reshape(rows_here, cols_here, CH, CH)
     left_whole = (

time: 250 us -> 282 us (1.13)
  waiting for transfers between devices: 85.4 us -> 109 us
  other arithmetic: 0.12 us -> 7.61 us
    psum x1 -> x0, waiting for transfers between devices: 85.4 us -> none  [shards(): proj_grad = lax.psum(weight_term, ('row', 'col'))]
    all_gather x0 -> x1, waiting for transfers between devices: none -> 70.9 us  [carry_weights(): odd = all_gather(shard_in, axis_name=row_axis)]
    reduce_scatter x1, waiting for transfers between devices: 0.01 us -> 38.5 us  [shards(): lax.psum_scatter(left_whole.reshape(seq_count, rows_here * CH), 'col', sc...]
    reduce_sum x0 -> x1, other arithmetic: none -> 7.48 us  [carry_weights(): y = jnp.sum(odd, axis=0)]
  transfers between devices with their start and end apart: 3 -> 3, of which waited for: 1 -> 2; matrix products, arithmetic and copies ran while one was open for 18% -> 19% of each run, Pallas kernels for 0% -> 0%
where the time goes in v1:
time: 282 us; the launch traced here: 280 us
  waiting for transfers between devices  109 us (39%)
  local copies, waits for them, and re-layouts  71 us (25%)
  blocking collectives  39.4 us (14%)
  matrix products  36.9 us (13%)
  between operations  15.5 us (5%)
  other arithmetic  7.61 us (3%)
    all_gather x1, waiting for transfers between devices, carry_weights(): odd = all_gather(shard_in, axis_name=row_axis)  70.9 us
    reduce_scatter x1, waiting for transfers between devices, shards(): lax.psum_scatter(left_whole.reshape(seq_count, rows_here * CH), 'col', sc...  38.5 us
    all_gather x1, blocking collectives, shards(): left_all = lax.all_gather(left, 'col', axis=0, tiled=True)  33.4 us
    convert_element_type x1, local copies, waits for them, and re-layouts, shards(): outers = square.astype(jnp.bfloat16).reshape(rows_here * cols_here, OUTER)  24.6 us
    reshape x1, local copies, waits for them, and re-layouts, shards(): outers = square.astype(jnp.bfloat16).reshape(rows_here * cols_here, OUTER)  23.3 us
    reshape x1, local copies, waits for them, and re-layouts, shards(): grad_cube = grad_outer.reshape(rows_here, cols_here, CH, CH)  20.3 us
    dot_general x1, matrix products, shards(): jnp.einsum('ijce,sic->sje', grad_cube, left_cube, preferred_element_type=...  10.3 us
    dot_general x1, matrix products, shards(): jnp.einsum('ijce,sje->sic', grad_cube, right_cube, preferred_element_type...  9.18 us
  transfers between devices with their start and end apart: 3, of which 2 were waited for; matrix products, arithmetic and copies ran while one was open for 19% of the time, Pallas kernels for 0%

profile of v1, /device:TPU:0, one launch (start us, length us, event | category | flops | bytes accessed | tf_op | source)
XLA Modules:
  0.0 280.1 jit_solution(9882330976459861286)
XLA Ops:
  8.0 0.0 all-gather.3.cloned.1.call-start
  8.1 33.4 %all_gather.13 = bf16[128,2048]{1,0:T(8,128)(2,1)S(1)} all-gather(bf16[16,2048]{1,0:T(8,128)(2,1)} %param.5), channel_id=1, replica_groups=mesh['row'=4,'col'=8] {'col'}, dimensions={0}, use_global_device_ids=true | all-gather | bytes 589824 | tf_op jit(solution)/shard_map/all_gather | solution.py:20
  41.4 0.3 copy.26
  41.7 6.0 %all_gather.12 = bf16[128,1024]{1,0:T(8,128)(2,1)S(1)} all-gather(bf16[32,1024]{1,0:T(8,128)(2,1)} %param.6), channel_id=1, replica_groups=mesh['row'=4,'col'=8] {'row'}, dimensions={0}, use_global_device_ids=true | all-gather | bytes 327680 | tf_op jit(solution)/shard_map/all_gather | solution.py:21
  47.7 0.2 copy.25
  47.9 5.6 %fusion = bf16[64,32,32,32]{0,3,2,1:T(8,128)(2,1)} fusion(bf16[128,32,32,1]{0,2,3,1:T(8,128)(2,1)S(1)} %bitcast.52, bf16[128,64,32]{0,2,1:T(8,128)(2,1)S(1)} %bitcast.50), kind=kOutput, calls=%fused_computation.1 | convolution fusion | flops 541065216 | bytes 4980736 | tf_op jit(solution)/shard_map/sic,sje->ijce/dot_general | solution.py:28
  53.5 24.6 %copy.28 = bf16[64,32,32,32]{3,2,1,0:T(8,128)(2,1)} copy(bf16[64,32,32,32]{0,3,2,1:T(8,128)(2,1)} %fusion) | data formatting | bytes 8388608 | tf_op jit(solution)/shard_map/convert_element_type | solution.py:31
  78.1 23.3 %reshape.36 = bf16[2048,1024]{1,0:T(8,128)(2,1)} reshape(bf16[64,32,32,32]{3,2,1,0:T(8,128)(2,1)} %copy.28) | data formatting | bytes 8388608 | tf_op jit(solution)/shard_map/reshape | solution.py:31
  101.4 0.1 convert_multiply_fusion
  101.6 4.2 %fusion.4 = (bf16[2048,128]{1,0:T(8,128)(2,1)S(1)}, bf16[2048,128]{1,0:T(8,128)(2,1)}) fusion(f32[64,32,128]{2,1,0:T(8,128)S(1)} %convert_multiply_fusion, f32[128]{0:T(128)S(1)} %copy-done.2, bf16[2048,1024]{1,0:T(8,128)(2,1)} %reshape.36, bf16[1024,128]{1,0:T(8,128)(2,1)S(1)} %copy-done), kind=kOutput, calls=%fused_computation.10 | convolution fusion | flops 538443776 | bytes 6554112 | tf_op jit(solution)/shard_map/dot_general | solution.py:32
  105.8 4.3 %fusion.7 = f32[1024,128]{1,0:T(8,128)} fusion(bf16[2048,1024]{1,0:T(8,128)(2,1)} %reshape.36, bf16[2048,128]{1,0:T(8,128)(2,1)S(1)} %get-tuple-element.4), kind=kOutput, calls=%fused_computation.15 | convolution fusion | flops 536870912 | bytes 5242880 | tf_op jit(solution)/shard_map/dot_general | solution.py:38
  110.1 0.2 reduce-scatter.5.cloned.1.call-start
  110.3 3.3 %convolution_convert_fusion = bf16[2048,1024]{1,0:T(8,128)(2,1)} fusion(bf16[2048,128]{1,0:T(8,128)(2,1)S(1)} %get-tuple-element.4, bf16[1024,128]{1,0:T(8,128)(2,1)S(1)} %copy-done), kind=kOutput, calls=%fused_computation.2 | convolution fusion | flops 538968064 | bytes 4980736 | tf_op jit(solution)/shard_map/dot_general | solution.py:42
  113.6 20.3 %reshape.38 = bf16[64,32,32,32]{3,2,1,0:T(8,128)(2,1)} reshape(bf16[2048,1024]{1,0:T(8,128)(2,1)} %convolution_convert_fusion) | data formatting | bytes 8388608 | tf_op jit(solution)/shard_map/reshape | solution.py:43
  133.9 10.3 %fusion.3 = f32[32,32,128]{2,1,0:T(8,128)S(1)} fusion(bf16[64,32,32,32]{3,2,1,0:T(8,128)(2,1)} %reshape.38, bf16[128,64,32,1]{0,2,3,1:T(8,128)(2,1)S(1)} %bitcast.51), kind=kOutput, calls=%fused_computation.8 | convolution fusion | flops 537001984 | bytes 5242880 | tf_op jit(solution)/shard_map/ijce,sic->sje/dot_general | solution.py:49
  144.2 1.0 copy.31
  145.2 0.0 reduce-scatter.5.cloned.1.call-update
  145.2 0.0 reduce-scatter.3.cloned.1.call-start
  145.3 9.2 %fusion.2 = f32[64,32,128]{2,1,0:T(8,128)S(1)} fusion(bf16[64,32,32,32]{3,2,1,0:T(8,128)(2,1)} %reshape.38, bf16[128,32,32,1]{0,2,1,3:T(8,128)(2,1)S(1)} %bitcast.53), kind=kOutput, calls=%fused_computation.6 | convolution fusion | flops 537133056 | bytes 5505024 | tf_op jit(solution)/shard_map/ijce,sje->sic/dot_general | solution.py:45
  154.5 1.3 copy.29
  155.8 0.0 reduce-scatter.3.cloned.1.call-update
  155.8 70.9 %all-gather.3.cloned.1.call-done = f32[32768,128]{1,0:T(8,128)} async-done(((f32[1024,128]{1,0:T(8,128)}), f32[32768,128]{1,0:T(8,128)}) %all-gather.3.cloned.1.call-update) | async-done | bytes 16777232 | tf_op jit(solution)/shard_map/all_gather | solution.py:14
  226.8 7.5 %reduce_sum.9 = f32[1024,128]{1,0:T(8,128)} reduce(f32[32,1024,128]{2,1,0:T(8,128)} %bitcast.49, f32[]{:T(128)} %constant.4.clone.1), dimensions={0}, to_apply=%region_2.0 | reduce | flops 4063232 | bytes 17301508 | tf_op jit(solution)/shard_map/reduce_sum | solution.py:15
  234.2 38.5 %reduce-scatter.3.cloned.1.call-done = f32[16,2048]{1,0:T(8,128)} async-done(((f32[128,2048]{1,0:T(8,128)}), f32[16,2048]{1,0:T(8,128)}) %reduce-scatter.3.cloned.1.call-update) | async-done | bytes 131088 | tf_op jit(solution)/shard_map/reduce_scatter | solution.py:51
  (8 shorter events, 0.0 us)
Async XLA Ops:
  8.0 93.6 %copy-start = (bf16[1024,128]{1,0:T(8,128)(2,1)S(1)}, bf16[1024,128]{1,0:T(8,128)(2,1)}, u32[]{:S(2)}) copy-start(bf16[1024,128]{1,0:T(8,128)(2,1)} %param.7) | copy-start | bytes 786436
  8.0 218.7 %all-gather.3.cloned.1.call-start = ((), (), s32[]{:S(2)}) async-start(), calls=%async_computation.4 | async-start | bytes 17301504 | tf_op jit(solution)/shard_map/all_gather | solution.py:14
  78.1 23.3 %copy-start.1 = (bf16[64,32,128]{2,1,0:T(8,128)(2,1)S(1)}, bf16[64,32,128]{2,1,0:T(8,128)(2,1)}, u32[]{:S(2)}) copy-start(bf16[64,32,128]{2,1,0:T(8,128)(2,1)} %param.9) | copy-start | bytes 1572868
  78.1 23.5 %copy-start.2 = (f32[128]{0:T(128)S(1)}, f32[128]{0:T(128)}, u32[]{:S(2)}) copy-start(f32[128]{0:T(128)} %param.8) | copy-start | bytes 1540
  110.1 124.1 %reduce-scatter.5.cloned.1.call-start = ((), (), s32[]{:S(2)}) async-start(), calls=%async_computation.3 | async-start | bytes 655360 | tf_op jit(solution)/shard_map/reduce_scatter | solution.py:54
  145.2 127.5 %reduce-scatter.3.cloned.1.call-start = ((), (), s32[]{:S(2)}) async-start(), calls=%async_computation.2 | async-start | bytes 1179648 | tf_op jit(solution)/shard_map/reduce_scatter | solution.py:51
Sparse Core Ops, SparseCore 0:
  110.2 116.4 all-gather.2
Sparse Core Ops, SparseCore 1:
  145.3 22.7 reduce-scatter.4
  171.9 100.8 reduce-scatter.2
